TPU v7x, 512 devices: a whole 4x4x16 slice. The times are simulated.
512 devices in a mesh: gy: 32 (over x, y, core), gz: 16 (over z).
Axes of the slice: x: 4, y: 4, z: 16, core: 2. Of those that a mesh axis runs over, the one named last changes fastest.
Arguments:
- volume: bfloat16 [64, 128, 64, 256], P(None, 'gy', 'gz'), may hold values from -2500 to 2500
- down_weight: bfloat16 [128, 64, 2, 2, 2], replicated, may hold values from -0.25 to 0.25
- conv_one: bfloat16 [3, 3, 128, 384], replicated, may hold values from -0.109375 to 0.109375
- conv_two: bfloat16 [3, 3, 128, 384], replicated, may hold values from -0.109375 to 0.109375
- norm_gain: float32 [3, 128], replicated, may hold values from 0.1 to 1.9
- norm_shift: float32 [3, 128], replicated, may hold values from -2.5 to 2.5
Outputs:
- features: bfloat16 [128, 64, 32, 128], P(None, 'gy', 'gz')
All inputs are finite; a program needn't handle non-finite values.
Results may differ from a plain program's by a relative error of at most 0.0065.
Values may be sent and summed in bfloat16 or wider, within the bound.
No kernel may reach another device: no remote copies, remote signals or barrier semaphores. Data moves between devices by JAX's collectives and lax.ppermute only.
A program may use at most 64 MiB of HBM per device.

v0:
```python
import jax
import jax.numpy as jnp
from jax import lax
from jax.sharding import PartitionSpec as P


def padded_2(value, sides, width):
    for axis, dim in sides:
        count, length = (lax.axis_size(axis), value.shape[dim])
        up = [(i, (i + 1) % count) for i in range(count - 1)]
        down = [(j, i) for i, j in up]
        last = lax.slice_in_dim(value, length - width, length, axis=dim)
        leading = lax.slice_in_dim(value, 0, width, axis=dim)
        before = lax.ppermute(last, axis, up)
        after = lax.ppermute(leading, axis, down)
        value = jnp.concatenate([before, value, after], axis=dim)
    return value


def leaky(value):
    return jnp.where(value >= 0.0, value, 0.01 * value)


def moments(inner):
    count = float(
        inner.shape[1] * inner.shape[2] * inner.shape[3] * lax.axis_size("gy") * lax.axis_size("gz")
    )
    total = lax.psum(jnp.sum(inner, axis=(1, 2, 3)), ("gy", "gz"))
    mean = total / count
    centered = inner - mean[:, None, None, None]
    spread = lax.psum(jnp.sum(centered * centered, axis=(1, 2, 3)), ("gy", "gz")) / count
    return (mean, spread)


def normalize(value, inner, gain, shift):
    mean, spread = moments(inner)
    scaled = (value - mean[:, None, None, None]) / jnp.sqrt(spread + 1e-05)[:, None, None, None]
    return leaky(scaled * gain[:, None, None, None] + shift[:, None, None, None])


def strided(volume, down_weight):
    blocks = volume.reshape(
        volume.shape[0], volume.shape[1] // 2, 2, volume.shape[2] // 2, 2, volume.shape[3] // 2, 2
    )
    return jnp.einsum(
        "oiabc,iyazbxc->oyzx", down_weight, blocks, preferred_element_type=jnp.float32
    )


def convolve(padded, conv_weight, rows, depth):
    length = padded.shape[3]
    widened = jnp.pad(padded, ((0, 0), (0, 0), (0, 0), (1, 1)))
    stacked = jnp.concatenate(
        [widened[:, :, :, offset : offset + length] for offset in range(3)], axis=0
    )
    total = jnp.zeros((conv_weight.shape[2], rows, depth, length), jnp.float32)
    for row_tap in range(3):
        for depth_tap in range(3):
            piece = stacked[:, row_tap : row_tap + rows, depth_tap : depth_tap + depth, :]
            total = total + jnp.einsum(
                "ok,kyzx->oyzx",
                conv_weight[row_tap, depth_tap],
                piece,
                preferred_element_type=jnp.float32,
            )
    return total


def faces(field):
    return padded_2(field, (("gy", 1), ("gz", 2)), 1)


def on_device(volume, down_weight, conv_one, conv_two, norm_gain, norm_shift):
    coarse = strided(volume, down_weight)
    rows = coarse.shape[1]
    depth = coarse.shape[2]
    first = normalize(coarse, coarse, norm_gain[0], norm_shift[0]).astype(jnp.bfloat16)
    middle = convolve(faces(first), conv_one, rows, depth)
    second = normalize(middle, middle, norm_gain[1], norm_shift[1]).astype(jnp.bfloat16)
    last = convolve(faces(second), conv_two, rows, depth)
    return normalize(last, last, norm_gain[2], norm_shift[2]).astype(jnp.bfloat16)


def solution(mesh):
    return jax.shard_map(
        on_device,
        mesh=mesh,
        in_specs=(P(None, "gy", "gz", None), P(), P(), P(), P(), P()),
        out_specs=P(None, "gy", "gz", None),
        check_vma=False,
    )
```

profile of v0, /device:TPU:1, one launch (start us, length us, event | category | flops | bytes accessed | tf_op | source)
XLA Modules:
  0.0 662.0 jit_solution(10334304953308035063)
XLA Ops:
  0.0 1.7 copy.10
  1.7 0.4 fusion.92
  2.1 111.0 %psum.42 = f32[128]{0:T(128)S(1)} all-reduce(f32[128]{0:T(128)S(1)} %get-tuple-element.23), channel_id=1, replica_groups=mesh['gy'=32,'gz'=16] {'gy','gz'}, use_global_device_ids=true, to_apply=%region_1.0 | all-reduce | flops 128 | bytes 1024 | tf_op jit(solution)/shard_map/psum | solution.py:28
  113.2 98.2 %psum.43 = f32[128]{0:T(128)S(1)} all-reduce(f32[128]{0:T(128)S(1)} %multiply_reduce_fusion.2), channel_id=1, replica_groups=mesh['gy'=32,'gz'=16] {'gy','gz'}, use_global_device_ids=true, to_apply=%region_3.0 | all-reduce | flops 128 | bytes 1024 | tf_op jit(solution)/shard_map/psum | solution.py:31
  211.6 2.9 collective-permute-start
  214.5 1.9 collective-permute-start.1
  216.4 3.6 collective-permute-done.1
  220.1 3.7 collective-permute-start.2
  223.8 1.3 collective-permute-start.3
  225.1 0.6 collective-permute-done.2
  225.7 3.8 collective-permute-done.3
  229.5 0.2 fusion.25
  229.7 0.3 fusion.87
  230.0 0.2 pad_maximum_fusion
  230.2 0.9 copy-done
  231.1 0.3 fusion.51
  231.4 0.3 fusion.53
  231.7 0.3 fusion.55
  231.9 0.3 fusion.57
  232.2 0.3 fusion.59
  232.5 0.3 fusion.61
  232.7 0.3 fusion.63
  233.0 0.3 fusion.65
  233.3 0.3 fusion.93
  233.6 102.8 %psum.44 = f32[128]{0:T(128)S(1)} all-reduce(f32[128]{0:T(128)S(1)} %get-tuple-element.25), channel_id=1, replica_groups=mesh['gy'=32,'gz'=16] {'gy','gz'}, use_global_device_ids=true, to_apply=%region_5.6 | all-reduce | flops 128 | bytes 1024 | tf_op jit(solution)/shard_map/psum | solution.py:28
  336.5 99.5 %psum.45 = f32[128]{0:T(128)S(1)} all-reduce(f32[128]{0:T(128)S(1)} %multiply_reduce_fusion.1), channel_id=1, replica_groups=mesh['gy'=32,'gz'=16] {'gy','gz'}, use_global_device_ids=true, to_apply=%region_7.8 | all-reduce | flops 128 | bytes 1024 | tf_op jit(solution)/shard_map/psum | solution.py:31
  436.1 3.4 collective-permute-start.4
  439.6 1.9 collective-permute-start.5
  441.5 3.6 collective-permute-done.5
  445.2 3.7 collective-permute-start.6
  448.9 1.3 collective-permute-start.7
  450.2 0.6 collective-permute-done.6
  450.8 3.8 collective-permute-done.7
  454.8 0.3 fusion.86
  455.1 0.2 pad_maximum_fusion.1
  455.3 0.9 copy-done.1
  456.3 0.3 fusion.34
  456.5 0.3 fusion.36
  456.8 0.3 fusion.38
  457.1 0.3 fusion.40
  457.3 0.3 fusion.42
  457.6 0.3 fusion.44
  457.9 0.3 fusion.46
  458.1 0.3 fusion.48
  458.4 0.3 fusion.94
  458.7 102.7 %psum.46 = f32[128]{0:T(128)S(1)} all-reduce(f32[128]{0:T(128)S(1)} %get-tuple-element.27), channel_id=1, replica_groups=mesh['gy'=32,'gz'=16] {'gy','gz'}, use_global_device_ids=true, to_apply=%region_9.10 | all-reduce | flops 128 | bytes 1024 | tf_op jit(solution)/shard_map/psum | solution.py:28
  561.5 99.5 %psum.47 = f32[128]{0:T(128)S(1)} all-reduce(f32[128]{0:T(128)S(1)} %multiply_reduce_fusion), channel_id=1, replica_groups=mesh['gy'=32,'gz'=16] {'gy','gz'}, use_global_device_ids=true, to_apply=%region_11.12 | all-reduce | flops 128 | bytes 1024 | tf_op jit(solution)/shard_map/psum | solution.py:31
  661.2 0.8 copy.13
  (30 shorter events, 0.9 us)
Async XLA Ops:
  0.0 1.7 copy-start.4
  0.0 211.4 %copy-start.2 = (f32[3,128]{1,0:T(4,128)S(1)}, f32[3,128]{1,0:T(4,128)}, u32[]{:S(2)}) copy-start(f32[3,128]{1,0:T(4,128)} %param.11) | copy-start | bytes 4612
  0.0 211.4 %copy-start.3 = (f32[3,128]{1,0:T(4,128)S(1)}, f32[3,128]{1,0:T(4,128)}, u32[]{:S(2)}) copy-start(f32[3,128]{1,0:T(4,128)} %param.10) | copy-start | bytes 4612
  211.6 4.8 collective-permute-start
  214.5 5.6 collective-permute-start.1
  220.1 5.6 collective-permute-start.2
  223.8 5.7 collective-permute-start.3
  230.0 1.2 copy-start
  436.1 5.4 collective-permute-start.4
  439.6 5.6 collective-permute-start.5
  445.2 5.6 collective-permute-start.6
  448.9 5.7 collective-permute-start.7
  455.1 1.2 copy-start.1
where the time goes:
time: 663 us; the launch traced here: 662 us
  blocking collectives  614 us (93%)
  starting transfers between devices  20.1 us (3%)
  waiting for transfers between devices  16.1 us (2%)
    psum x3, blocking collectives, moments(): total = lax.psum(jnp.sum(inner, axis=(1, 2, 3)), ('gy', 'gz'))  317 us
    psum x3, blocking collectives, moments(): lax.psum(jnp.sum(centered * centered, axis=(1, 2, 3)), ('gy', 'gz')) / count  297 us
    ppermute x4, waiting for transfers between devices, padded_2(): after = lax.ppermute(leading, axis, down)  14.9 us
    ppermute x4, starting transfers between devices, padded_2(): before = lax.ppermute(last, axis, up)  13.7 us
  transfers between devices with their start and end apart: 8, of which 6 were waited for; matrix products, arithmetic and copies ran while one was open for 0% of the time, Pallas kernels for 0%

commit v1 on v0

--- a/solution.py
+++ b/solution.py
@@ -2,6 +2,10 @@
 import jax.numpy as jnp
 from jax import lax
 from jax.sharding import PartitionSpec as P
+
+_move_floor = lambda mine, lane_axis, group_axis: lax.psum(
+    lax.psum(mine, axis_name=lane_axis), axis_name=group_axis
+)
 
 
 def padded_2(value, sides, width):
@@ -25,7 +29,7 @@
     count = float(
         inner.shape[1] * inner.shape[2] * inner.shape[3] * lax.axis_size("gy") * lax.axis_size("gz")
     )
-    total = lax.psum(jnp.sum(inner, axis=(1, 2, 3)), ("gy", "gz"))
+    total = _move_floor(jnp.sum(inner, axis=(1, 2, 3)), "gz", "gy")
     mean = total / count
     centered = inner - mean[:, None, None, None]
     spread = lax.psum(jnp.sum(centered * centered, axis=(1, 2, 3)), ("gy", "gz")) / count

time: 663 us -> 624 us (0.941)
  blocking collectives: 614 us -> 577 us
    psum x3 -> x6, blocking collectives: 317 us -> 280 us  [the longest x3 206 us: lax.psum(lax.psum(mine, axis_name=lane_axis), axis_name=group_axis)]
where the time goes in v1:
time: 624 us; the launch traced here: 623 us
  blocking collectives  577 us (92%)
  starting transfers between devices  18.6 us (3%)
  waiting for transfers between devices  15.6 us (2%)
    psum x3, blocking collectives, moments(): lax.psum(jnp.sum(centered * centered, axis=(1, 2, 3)), ('gy', 'gz')) / count  296 us
    psum x3, blocking collectives, lax.psum(lax.psum(mine, axis_name=lane_axis), axis_name=group_axis)  206 us
    psum x3, blocking collectives, lax.psum(mine, axis_name=lane_axis)  74.4 us
    ppermute x4, waiting for transfers between devices, padded_2(): after = lax.ppermute(leading, axis, down)  14.3 us
  transfers between devices with their start and end apart: 8, of which 6 were waited for; matrix products, arithmetic and copies ran while one was open for 0% of the time, Pallas kernels for 0%

profile of v1, /device:TPU:1, one launch (start us, length us, event | category | flops | bytes accessed | tf_op | source)
XLA Modules:
  0.0 622.8 jit_solution(9052674596972739174)
XLA Ops:
  0.0 1.7 copy.10
  1.7 0.4 fusion.92
  2.1 30.3 %psum.63 = f32[128]{0:T(128)S(1)} all-reduce(f32[128]{0:T(128)S(1)} %get-tuple-element.23), channel_id=1, replica_groups=mesh['gy'=32,'gz'=16] {'gz'}, use_global_device_ids=true, to_apply=%region_1.0 | all-reduce | flops 128 | bytes 1024 | tf_op jit(solution)/shard_map/psum | solution.py:7
  32.4 69.9 %psum.64 = f32[128]{0:T(128)S(1)} all-reduce(f32[128]{0:T(128)S(1)} %psum.63), channel_id=1, replica_groups=mesh['gy'=32,'gz'=16] {'gy'}, use_global_device_ids=true, to_apply=%region_2.0 | all-reduce | flops 128 | bytes 1024 | tf_op jit(solution)/shard_map/psum | solution.py:6
  102.4 98.7 %psum.65 = f32[128]{0:T(128)S(1)} all-reduce(f32[128]{0:T(128)S(1)} %multiply_reduce_fusion.2), channel_id=1, replica_groups=mesh['gy'=32,'gz'=16] {'gy','gz'}, use_global_device_ids=true, to_apply=%region_4.0 | all-reduce | flops 128 | bytes 1024 | tf_op jit(solution)/shard_map/psum | solution.py:35
  201.3 1.9 collective-permute-start
  203.2 2.4 collective-permute-start.1
  205.7 3.2 collective-permute-done.1
  208.9 3.7 collective-permute-start.2
  212.6 1.3 collective-permute-start.3
  213.9 0.6 collective-permute-done.2
  214.5 4.0 collective-permute-done.3
  218.7 0.3 fusion.87
  219.2 0.9 copy-done
  220.1 0.3 fusion.51
  220.4 0.3 fusion.53
  220.6 0.3 fusion.55
  220.9 0.3 fusion.57
  221.2 0.3 fusion.59
  221.5 0.3 fusion.61
  221.7 0.3 fusion.63
  222.0 0.3 fusion.65
  222.3 0.3 fusion.93
  222.6 21.4 %psum.66 = f32[128]{0:T(128)S(1)} all-reduce(f32[128]{0:T(128)S(1)} %get-tuple-element.25), channel_id=1, replica_groups=mesh['gy'=32,'gz'=16] {'gz'}, use_global_device_ids=true, to_apply=%region_6.7 | all-reduce | flops 128 | bytes 1024 | tf_op jit(solution)/shard_map/psum | solution.py:7
  244.0 68.2 %psum.67 = f32[128]{0:T(128)S(1)} all-reduce(f32[128]{0:T(128)S(1)} %psum.66), channel_id=1, replica_groups=mesh['gy'=32,'gz'=16] {'gy'}, use_global_device_ids=true, to_apply=%region_7.8 | all-reduce | flops 128 | bytes 1024 | tf_op jit(solution)/shard_map/psum | solution.py:6
  312.3 98.8 %psum.68 = f32[128]{0:T(128)S(1)} all-reduce(f32[128]{0:T(128)S(1)} %multiply_reduce_fusion.1), channel_id=1, replica_groups=mesh['gy'=32,'gz'=16] {'gy','gz'}, use_global_device_ids=true, to_apply=%region_9.10 | all-reduce | flops 128 | bytes 1024 | tf_op jit(solution)/shard_map/psum | solution.py:35
  411.2 2.1 collective-permute-start.4
  413.3 2.2 collective-permute-start.5
  415.6 3.3 collective-permute-done.5
  419.0 3.7 collective-permute-start.6
  422.7 1.3 collective-permute-start.7
  424.0 0.6 collective-permute-done.6
  424.6 3.8 collective-permute-done.7
  428.6 0.3 fusion.86
  429.1 0.9 copy-done.1
  430.0 0.3 fusion.34
  430.3 0.3 fusion.36
  430.6 0.3 fusion.38
  430.8 0.3 fusion.40
  431.1 0.3 fusion.42
  431.4 0.3 fusion.44
  431.7 0.3 fusion.46
  431.9 0.3 fusion.48
  432.2 0.3 fusion.94
  432.5 22.6 %psum.69 = f32[128]{0:T(128)S(1)} all-reduce(f32[128]{0:T(128)S(1)} %get-tuple-element.27), channel_id=1, replica_groups=mesh['gy'=32,'gz'=16] {'gz'}, use_global_device_ids=true, to_apply=%region_11.12 | all-reduce | flops 128 | bytes 1024 | tf_op jit(solution)/shard_map/psum | solution.py:7
  455.1 67.9 %psum.70 = f32[128]{0:T(128)S(1)} all-reduce(f32[128]{0:T(128)S(1)} %psum.69), channel_id=1, replica_groups=mesh['gy'=32,'gz'=16] {'gy'}, use_global_device_ids=true, to_apply=%region_12.13 | all-reduce | flops 128 | bytes 1024 | tf_op jit(solution)/shard_map/psum | solution.py:6
  523.2 98.8 %psum.71 = f32[128]{0:T(128)S(1)} all-reduce(f32[128]{0:T(128)S(1)} %multiply_reduce_fusion), channel_id=1, replica_groups=mesh['gy'=32,'gz'=16] {'gy','gz'}, use_global_device_ids=true, to_apply=%region_14.15 | all-reduce | flops 128 | bytes 1024 | tf_op jit(solution)/shard_map/psum | solution.py:35
  622.0 0.8 copy.13
  (33 shorter events, 1.5 us)
Async XLA Ops:
  0.0 1.7 copy-start.4
  0.0 201.2 %copy-start.2 = (f32[3,128]{1,0:T(4,128)S(1)}, f32[3,128]{1,0:T(4,128)}, u32[]{:S(2)}) copy-start(f32[3,128]{1,0:T(4,128)} %param.11) | copy-start | bytes 4612
  0.0 201.2 %copy-start.3 = (f32[3,128]{1,0:T(4,128)S(1)}, f32[3,128]{1,0:T(4,128)}, u32[]{:S(2)}) copy-start(f32[3,128]{1,0:T(4,128)} %param.10) | copy-start | bytes 4612
  201.3 4.3 collective-permute-start
  203.2 5.6 collective-permute-start.1
  208.9 5.6 collective-permute-start.2
  212.6 5.9 collective-permute-start.3
  218.9 1.2 copy-start
  411.2 4.3 collective-permute-start.4
  413.3 5.6 collective-permute-start.5
  419.0 5.6 collective-permute-start.6
  422.7 5.8 collective-permute-start.7
  428.9 1.2 copy-start.1
